TPU v7x, 128 devices: a whole 4x4x4 slice. The times are simulated.
128 devices in a mesh: row: 8 (over x_lo, y), col: 16 (over x_hi, z, core).
Axes of the slice: x: 4 (x_hi: 2, x_lo: 2; x = x_hi * 2 + x_lo), y: 4, z: 4, core: 2. Of those that a mesh axis runs over, the one named last changes fastest.
Arguments:
- query_acts: bfloat16 [2048, 6144], P('col', 'row'), may hold values from -6 to 6
- query_grads: bfloat16 [2048, 6144], P('row', 'col'), may hold values from -6 to 6
- act_basis: bfloat16 [6144, 6144], P('row', 'col'), may hold values from -0.078125 to 0.078125
- grad_basis: bfloat16 [6144, 6144], P('col', 'row'), may hold values from -0.078125 to 0.078125
- eigenvalues: float32 [6144, 6144], P('row', 'col'), may hold values from 0.05 to 5
- train_acts: bfloat16 [2560, 6144], P('row', 'col'), may hold values from -6 to 6
- train_grads: bfloat16 [2560, 6144], P('col', 'row'), may hold values from -6 to 6
Outputs:
- scores: float32 [8, 2560], P(None, ('row', 'col'))
All inputs are finite; a program needn't handle non-finite values.
Results may differ from a plain program's by a relative error of at most 0.012.
Values may be sent and summed in bfloat16 or wider, within the bound.
A program may use at most 64 MiB of HBM per device.

v0:
```python
import jax
import jax.numpy as jnp
from jax import lax
from jax.sharding import PartitionSpec as P

D = 6144
QUERY_LEN = 256


damping = 0.01


def tile_scores(panels, act_rows, grad_rows):

    def per_query(panel):
        mapped = lax.dot_general(
            act_rows, panel, (((1,), (1,)), ((), ())), preferred_element_type=jnp.float32
        )
        return jnp.sum(mapped * grad_rows, axis=1)

    return lax.map(per_query, panels)


def shards(query_acts, query_grads, act_basis, grad_basis, eigenvalues, train_acts, train_grads):
    acts_in = lax.all_gather(query_acts, "col", axis=0, tiled=True)
    grads_in = lax.all_gather(query_grads, "row", axis=0, tiled=True)
    acts_part = jnp.dot(acts_in, act_basis, preferred_element_type=jnp.float32)
    grads_part = jnp.dot(grads_in, grad_basis, preferred_element_type=jnp.float32)
    rot_acts = lax.psum(acts_part, "row").astype(jnp.bfloat16)
    rot_grads = lax.psum(grads_part, "col").astype(jnp.bfloat16)
    queries = rot_acts.shape[0] // QUERY_LEN
    grads_q = rot_grads.reshape(queries, QUERY_LEN, rot_grads.shape[1])
    acts_q = rot_acts.reshape(queries, QUERY_LEN, rot_acts.shape[1])
    outer = jnp.einsum("qti,qtj->qij", grads_q, acts_q, preferred_element_type=jnp.float32)
    panels = (outer / (QUERY_LEN * (eigenvalues + damping))).astype(jnp.bfloat16)
    grads_all = lax.all_gather(train_grads, "col", axis=0, tiled=True)
    partial_value = tile_scores(
        panels, lax.all_gather(train_acts, "row", axis=0, tiled=True), grads_all
    )
    partial_value = partial_value / D
    scores = lax.psum_scatter(partial_value, ("row", "col"), scatter_dimension=1, tiled=True)
    return scores


def solution(mesh):
    return jax.shard_map(
        shards,
        mesh=mesh,
        in_specs=(
            P("col", "row"),
            P("row", "col"),
            P("row", "col"),
            P("col", "row"),
            P("row", "col"),
            P("row", "col"),
            P("col", "row"),
        ),
        out_specs=P(None, ("row", "col")),
        check_vma=False,
    )
```

profile of v0, /device:TPU:1, one launch (start us, length us, event | category | flops | bytes accessed | tf_op | source)
XLA Modules:
  0.0 466.4 jit_solution(11259363009860994968)
XLA Ops:
  6.5 0.0 copy-start
  6.5 0.0 all-gather.5.cloned.1.call-start
  6.5 0.7 all-gather.5.cloned.1.call-update
  7.3 0.0 all-gather.7.cloned.1.call-start
  7.3 0.7 all-gather.7.cloned.1.call-update
  8.0 0.0 all-gather.11.cloned.1.call-start
  8.1 0.7 all-gather.11.cloned.1.call-update
  8.7 0.0 all-gather.9.cloned.1.call-start
  8.8 0.5 all-gather.9.cloned.1.call-update
  9.3 0.0 all-reduce.5.cloned.1.call-start
  9.4 1.4 add_multiply_fusion
  10.8 35.8 %all-gather.5.cloned.1.call-done = bf16[2048,384]{1,0:T(8,128)(2,1)} async-done(((bf16[256,384]{1,0:T(8,128)(2,1)}), bf16[2048,384]{1,0:T(8,128)(2,1)}) %all-gather.5.cloned.1.call-update) | async-done | bytes 1572880 | tf_op jit(solution)/shard_map/all_gather | solution.py:26
  46.6 0.0 copy-done
  46.6 5.9 %fusion.4 = f32[2048,768]{1,0:T(8,128)} fusion(bf16[2048,384]{1,0:T(8,128)(2,1)} %all-gather.5.cloned.1.call-done, bf16[384,768]{1,0:T(8,128)(2,1)S(1)} %copy-done), kind=kOutput, calls=%fused_computation.9 | convolution fusion | flops 1207959552 | bytes 8454144 | tf_op jit(solution)/shard_map/dot_general | solution.py:28
  52.5 0.0 copy-start.1
  52.5 111.2 %all-reduce.6 = bf16[2048,768]{1,0:T(8,128)(2,1)} all-reduce(f32[2048,768]{1,0:T(8,128)} %fusion.4), channel_id=1, replica_groups=mesh['row'=8,'col'=16] {'col'}, use_global_device_ids=true, to_apply=%region_0.0 | all-reduce | flops 1572864 | bytes 9437184 | tf_op jit(solution)/shard_map/psum | solution.py:30
  163.7 0.0 all-gather.7.cloned.1.call-done
  163.7 0.0 copy-done.1
  163.7 5.3 %fusion.5 = f32[2048,384]{1,0:T(8,128)} fusion(bf16[2048,768]{1,0:T(8,128)(2,1)} %all-gather.7.cloned.1.call-done, bf16[768,384]{1,0:T(8,128)(2,1)S(1)} %copy-done.1), kind=kOutput, calls=%fused_computation.10 | convolution fusion | flops 1207959552 | bytes 6881280 | tf_op jit(solution)/shard_map/dot_general | solution.py:27
  169.0 89.3 %all-reduce.7 = bf16[2048,384]{1,0:T(8,128)(2,1)S(1)} all-reduce(f32[2048,384]{1,0:T(8,128)} %fusion.5), channel_id=1, replica_groups=mesh['row'=8,'col'=16] {'row'}, use_global_device_ids=true, to_apply=%region_1.0 | all-reduce | flops 786432 | bytes 4718592 | tf_op jit(solution)/shard_map/psum | solution.py:29
  258.3 5.9 %divide_convert_fusion = bf16[8,768,384]{2,1,0:T(8,128)(2,1)} fusion(f32[768,384]{1,0:T(8,128)S(1)} %add_multiply_fusion, bf16[8,256,768]{2,1,0:T(8,128)(2,1)} %bitcast.24, bf16[8,256,384]{2,1,0:T(8,128)(2,1)S(1)} %bitcast.25), kind=kOutput, calls=%fused_computation.5 | convolution fusion | flops 1212678144 | bytes 10616832 | tf_op jit(solution)/shard_map/qti,qtj->qij/dot_general | solution.py:34
  264.2 0.0 all-gather.11.cloned.1.call-done
  264.2 6.3 %copy.11 = bf16[2560,768]{0,1:T(8,128)(2,1)} copy(bf16[2560,768]{1,0:T(8,128)(2,1)} %all-gather.11.cloned.1.call-done) | data formatting | bytes 7864320 | tf_op jit(solution)/shard_map/while | solution.py:21
  270.5 0.0 all-gather.9.cloned.1.call-done
  270.5 43.5 %while.10 = (s32[]{:T(128)}, f32[8,2560]{1,0:T(8,128)S(1)}, bf16[8,768,384]{2,1,0:T(8,128)(2,1)}, bf16[2560,384]{1,0:T(8,128)(2,1)}, bf16[2560,768]{0,1:T(8,128)(2,1)}, /*index=5*/s32[]{:T(128)}, s32[]{:T(128)}) while((s32[]{:T(128)}, f32[8,2560]{1,0:T(8,128)S(1)}, bf16[8,768,384]{2,1,0:T(8,128)(2,1)}, bf16[2560,384]{1,0:T(8,128)(2,1)}, ...), condition=%wide.region_4.5_spmd, body=%wide.region_2.4_spmd.sunk | while | flops 1515845120 | bytes 6539857 | solution.py:21
  270.5 5.2 %fusion.18 = f32[2560]{0:T(1024)S(1)} fusion(bf16[2560,768]{0,1:T(8,128)(2,1)} %get-tuple-element.97, bf16[2560,384]{1,0:T(8,128)(2,1)} %get-tuple-element.96, bf16[8,768,384]{2,1,0:T(8,128)(2,1)} %get-tuple-element.95, s32[]{:T(128)} %get-tuple-element.86), kind=kOutput, calls=%fused_computation.1.clone.1 | convolution fusion | flops 1515845120 | bytes 6498816 | tf_op jit(solution)/shard_map/while/body/eval_jaxpr/dot_general | solution.py:16
  275.7 0.3 dynamic_update_slice.5
  276.0 5.2 %fusion.18 = f32[2560]{0:T(1024)S(1)} fusion(bf16[2560,768]{0,1:T(8,128)(2,1)} %get-tuple-element.97, bf16[2560,384]{1,0:T(8,128)(2,1)} %get-tuple-element.96, bf16[8,768,384]{2,1,0:T(8,128)(2,1)} %get-tuple-element.95, s32[]{:T(128)} %get-tuple-element.86), kind=kOutput, calls=%fused_computation.1.clone.1 | convolution fusion | flops 1515845120 | bytes 6498816 | tf_op jit(solution)/shard_map/while/body/eval_jaxpr/dot_general | solution.py:16
  281.2 0.3 dynamic_update_slice.5
  281.4 5.2 %fusion.18 = f32[2560]{0:T(1024)S(1)} fusion(bf16[2560,768]{0,1:T(8,128)(2,1)} %get-tuple-element.97, bf16[2560,384]{1,0:T(8,128)(2,1)} %get-tuple-element.96, bf16[8,768,384]{2,1,0:T(8,128)(2,1)} %get-tuple-element.95, s32[]{:T(128)} %get-tuple-element.86), kind=kOutput, calls=%fused_computation.1.clone.1 | convolution fusion | flops 1515845120 | bytes 6498816 | tf_op jit(solution)/shard_map/while/body/eval_jaxpr/dot_general | solution.py:16
  286.6 0.3 dynamic_update_slice.5
  286.9 5.1 %fusion.18 = f32[2560]{0:T(1024)S(1)} fusion(bf16[2560,768]{0,1:T(8,128)(2,1)} %get-tuple-element.97, bf16[2560,384]{1,0:T(8,128)(2,1)} %get-tuple-element.96, bf16[8,768,384]{2,1,0:T(8,128)(2,1)} %get-tuple-element.95, s32[]{:T(128)} %get-tuple-element.86), kind=kOutput, calls=%fused_computation.1.clone.1 | convolution fusion | flops 1515845120 | bytes 6498816 | tf_op jit(solution)/shard_map/while/body/eval_jaxpr/dot_general | solution.py:16
  292.0 0.3 dynamic_update_slice.5
  292.3 5.1 %fusion.18 = f32[2560]{0:T(1024)S(1)} fusion(bf16[2560,768]{0,1:T(8,128)(2,1)} %get-tuple-element.97, bf16[2560,384]{1,0:T(8,128)(2,1)} %get-tuple-element.96, bf16[8,768,384]{2,1,0:T(8,128)(2,1)} %get-tuple-element.95, s32[]{:T(128)} %get-tuple-element.86), kind=kOutput, calls=%fused_computation.1.clone.1 | convolution fusion | flops 1515845120 | bytes 6498816 | tf_op jit(solution)/shard_map/while/body/eval_jaxpr/dot_general | solution.py:16
  297.5 0.3 dynamic_update_slice.5
  297.7 5.1 %fusion.18 = f32[2560]{0:T(1024)S(1)} fusion(bf16[2560,768]{0,1:T(8,128)(2,1)} %get-tuple-element.97, bf16[2560,384]{1,0:T(8,128)(2,1)} %get-tuple-element.96, bf16[8,768,384]{2,1,0:T(8,128)(2,1)} %get-tuple-element.95, s32[]{:T(128)} %get-tuple-element.86), kind=kOutput, calls=%fused_computation.1.clone.1 | convolution fusion | flops 1515845120 | bytes 6498816 | tf_op jit(solution)/shard_map/while/body/eval_jaxpr/dot_general | solution.py:16
  302.9 0.3 dynamic_update_slice.5
  303.2 5.1 %fusion.18 = f32[2560]{0:T(1024)S(1)} fusion(bf16[2560,768]{0,1:T(8,128)(2,1)} %get-tuple-element.97, bf16[2560,384]{1,0:T(8,128)(2,1)} %get-tuple-element.96, bf16[8,768,384]{2,1,0:T(8,128)(2,1)} %get-tuple-element.95, s32[]{:T(128)} %get-tuple-element.86), kind=kOutput, calls=%fused_computation.1.clone.1 | convolution fusion | flops 1515845120 | bytes 6498816 | tf_op jit(solution)/shard_map/while/body/eval_jaxpr/dot_general | solution.py:16
  308.3 0.3 dynamic_update_slice.5
  308.6 5.1 %fusion.18 = f32[2560]{0:T(1024)S(1)} fusion(bf16[2560,768]{0,1:T(8,128)(2,1)} %get-tuple-element.97, bf16[2560,384]{1,0:T(8,128)(2,1)} %get-tuple-element.96, bf16[8,768,384]{2,1,0:T(8,128)(2,1)} %get-tuple-element.95, s32[]{:T(128)} %get-tuple-element.86), kind=kOutput, calls=%fused_computation.1.clone.1 | convolution fusion | flops 1515845120 | bytes 6498816 | tf_op jit(solution)/shard_map/while/body/eval_jaxpr/dot_general | solution.py:16
  313.8 0.3 dynamic_update_slice.5
  314.0 0.6 broadcast_multiply_fusion
  314.7 0.0 all-reduce.5.cloned.1.call-update
  314.7 143.8 %all-reduce.5.cloned.1.call-done = f32[8,2560]{1,0:T(8,128)} async-done(((f32[8,2560]{1,0:T(8,128)}), f32[8,2560]{1,0:T(8,128)}) %all-reduce.5.cloned.1.call-update) | async-done | bytes 81936
  458.5 1.4 constant_dynamic-slice_fusion
  (9 shorter events, 0.1 us)
Async XLA Ops:
  6.5 40.1 %copy-start = (bf16[384,768]{1,0:T(8,128)(2,1)S(1)}, bf16[384,768]{1,0:T(8,128)(2,1)}, u32[]{:S(2)}) copy-start(bf16[384,768]{1,0:T(8,128)(2,1)} %param.12) | copy-start | bytes 1769476
  6.5 40.1 %all-gather.5.cloned.1.call-start = ((), (), s32[]{:S(2)}) async-start(), calls=%async_computation | async-start | bytes 1769472 | tf_op jit(solution)/shard_map/all_gather | solution.py:26
  7.3 156.4 %all-gather.7.cloned.1.call-start = ((), (), s32[]{:S(2)}) async-start(), calls=%async_computation.1 | async-start | bytes 3342336 | tf_op jit(solution)/shard_map/all_gather | solution.py:25
  8.0 256.2 %all-gather.11.cloned.1.call-start = ((), (), s32[]{:S(2)}) async-start(), calls=%async_computation.3 | async-start | bytes 4177920 | tf_op jit(solution)/shard_map/all_gather | solution.py:36
  8.7 261.8 %all-gather.9.cloned.1.call-start = ((), (), s32[]{:S(2)}) async-start(), calls=%async_computation.2 | async-start | bytes 2211840 | tf_op jit(solution)/shard_map/all_gather | solution.py:38
  9.3 449.2 %all-reduce.5.cloned.1.call-start = ((), (), s32[]{:S(2)}) async-start(), calls=%async_computation.4 | async-start | bytes 163840
  52.5 111.2 %copy-start.1 = (bf16[768,384]{1,0:T(8,128)(2,1)S(1)}, bf16[768,384]{1,0:T(8,128)(2,1)}, u32[]{:S(2)}) copy-start(bf16[768,384]{1,0:T(8,128)(2,1)} %param.11) | copy-start | bytes 1769476
Sparse Core Ops, SparseCore 0:
  9.0 37.5 all-gather.4
  49.1 78.1 all-gather.6
  129.8 68.4 all-gather.10
  199.7 47.4 all-gather.8
  314.8 143.6 all-reduce.4
where the time goes:
time: 467 us; the launch traced here: 466 us
  blocking collectives  200 us (43%)
  waiting for transfers between devices  182 us (39%)
  matrix products  58.2 us (12%)
  between operations  13.2 us (3%)
  local copies, waits for them, and re-layouts  9.78 us (2%)
    unnamed x6, waiting for transfers between devices  146 us
    psum x1, blocking collectives, shards(): rot_grads = lax.psum(grads_part, 'col').astype(jnp.bfloat16)  111 us
    psum x1, blocking collectives, shards(): rot_acts = lax.psum(acts_part, 'row').astype(jnp.bfloat16)  89.3 us
    dot_general x8, matrix products, per_query(): lax.dot_general(act_rows, panel, (((1,), (1,)), ((), ())), preferred_elem...  41.1 us
    all_gather x1, waiting for transfers between devices, shards(): grads_in = lax.all_gather(query_grads, 'row', axis=0, tiled=True)  35.8 us
  transfers between devices with their start and end apart: 5, of which 2 were waited for; matrix products, arithmetic and copies ran while one was open for 5% of the time, Pallas kernels for 0%

commit v1 on v0

v1 whole, which is shorter than its diff:
```python
import jax
import jax.numpy as jnp
from jax import lax
from jax.experimental import pallas as pl
from jax.experimental.pallas import tpu as pltpu
from jax.sharding import PartitionSpec as P

D = 6144
QUERY_LEN = 256
QUERIES = 8
DAMPING = 0.01

ROWS = 8
COLS = 16
TILE_I = D // ROWS
TILE_J = D // COLS
TOKENS = QUERIES * QUERY_LEN
TRAIN = 2560
BLOCK = TRAIN // 8
OWNED = TRAIN // (ROWS * COLS)

CHUNKS = 4
PER_CHUNK = QUERIES // CHUNKS
CHUNK_TOKENS = PER_CHUNK * QUERY_LEN
PIECE = CHUNK_TOKENS // 4
HALF = PIECE // 2

MESH = pl.DeviceIdType.MESH
BF16 = jnp.bfloat16
F32 = jnp.float32

AG_A, AG_G, AG_TA, AG_TG = 0, 9, 18, 27
SIB_A, SIB_G, SIB_TG = 36, 44, 52
SIB_BASIS = 60
REDUCE = 61
PER_REDUCE = 10
FIRST = REDUCE + 2 * CHUNKS * PER_REDUCE
SECOND = FIRST + ROWS - 1
N_SEMS = SECOND + COLS - 1


def kernel(
    qa_ref, qg_ref, ab_ref, gb_ref, eig_ref, ta_ref, tg_ref, out_ref,
    qa, qg, ab, gb, rcp, ta, tg, part, rot_a, rot_g, near, mid, mine, other,
    panels, acc, first, split, second, local, sent, got,
):
    r = lax.axis_index("row")
    c = lax.axis_index("col")
    xl, y = r // 4, r % 4
    xh, z, k = c // 8, (c // 2) % 4, c % 2
    sib = (r, c + 1 - 2 * k)

    class Group:
        pass

    row_g, col_g = Group(), Group()
    row_g.p, row_g.u = xl, y
    row_g.up, row_g.dn = (xl * 4 + (y + 1) % 4, c), (xl * 4 + (y + 3) % 4, c)
    row_g.pair = ((1 - xl) * 4 + y, c)
    col_g.p, col_g.u = xh, z
    col_g.up = (r, xh * 8 + ((z + 1) % 4) * 2 + k)
    col_g.dn = (r, xh * 8 + ((z + 3) % 4) * 2 + k)
    col_g.pair = (r, (1 - xh) * 8 + z * 2 + k)

    def remote(src, dst, i, dev):
        return pltpu.make_async_remote_copy(
            src_ref=src, dst_ref=dst, send_sem=sent.at[i], recv_sem=got.at[i],
            device_id=dev, device_id_type=MESH,
        )

    def lanes(core):
        return pl.ds(pl.multiple_of(core * TILE_J, TILE_J), TILE_J)

    def rows_of(ref, core, size):
        def view(slot, lo, n):
            return ref.at[slot, pl.ds(pl.multiple_of(core * size + lo, 16), n)]

        return view

    def lanes_of(ref, core):
        def view(slot, lo, n):
            return ref.at[slot, pl.ds(lo, n), lanes(core)]

        return view

    def whole(ref):
        def view(slot, lo, n):
            return ref.at[slot, pl.ds(lo, n)]

        return view

    class Gather:
        def __init__(self, g, src, view, view_sib, n, base, sib_base):
            self.g, self.src, self.view, self.view_sib = g, src, view, view_sib
            self.n, self.base, self.sib_base = n, base, sib_base
            p, u = g.p, g.u
            self.own, self.q1 = p * 4 + u, (1 - p) * 4 + u
            m, o, w = (u + 3) % 4, (u + 1) % 4, (u + 2) % 4
            self.low = (p * 4 + m, (1 - p) * 4 + m)
            self.high = (p * 4 + o, (1 - p) * 4 + o)
            self.far = (p * 4 + w, (1 - p) * 4 + w)

        def full(self, slot):
            return self.view(slot, 0, self.n)

        def half(self, slot, h):
            return self.view(slot, h * (self.n // 2), self.n // 2)

        def copies(self, stage):
            g, b = self.g, self.base
            if stage == "pair":
                return [(self.src, self.full(self.own), b, g.pair)]
            if stage == "near0":
                return [
                    (self.src, self.full(self.own), b + 1, g.up),
                    (self.src, self.full(self.own), b + 2, g.dn),
                ]
            if stage == "near1":
                v = self.full(self.q1)
                return [(v, v, b + 3, g.up), (v, v, b + 4, g.dn)]
            i = 0 if stage == "far0" else 1
            lo, hi = self.half(self.low[i], 0), self.half(self.high[i], 1)
            return [(lo, lo, b + 5 + 2 * i, g.up), (hi, hi, b + 6 + 2 * i, g.dn)]

        def start(self, stage):
            for a in self.copies(stage):
                remote(*a).start()

        def wait_send(self):
            for stage in ("pair", "near0", "near1", "far0", "far1"):
                for a in self.copies(stage):
                    remote(*a).wait_send()

        def wait(self, stage):
            b, g = self.base, self.g
            if stage == "pair":
                got_ = [(self.full(self.q1), b, g.pair)]
            elif stage in ("near0", "near1"):
                i = 0 if stage == "near0" else 1
                got_ = [
                    (self.full(self.low[i]), b + 1 + 2 * i, g.dn),
                    (self.full(self.high[i]), b + 2 + 2 * i, g.up),
                ]
            else:
                i = 0 if stage == "far0" else 1
                got_ = [
                    (self.half(self.far[i], 0), b + 5 + 2 * i, g.dn),
                    (self.half(self.far[i], 1), b + 6 + 2 * i, g.up),
                ]
            for v, i, dev in got_:
                remote(v, v, i, dev).wait_recv()

        def slots(self):
            return (
                self.own, self.q1, self.low[0], self.high[0],
                self.low[1], self.high[1], self.far[0], self.far[1],
            )

        def sib_copy(self, j):
            slot = self.slots()[j]
            src = self.src if j == 0 else self.full(slot)
            return remote(src, self.full(slot), self.sib_base + j, sib)

        def sib_start(self, *js):
            for j in js:
                self.sib_copy(j).start()

        def sib_wait(self):
            for j, slot in enumerate(self.slots()):
                v = self.view_sib(slot, 0, self.n)
                remote(v, v, self.sib_base + j, sib).wait_recv()

        def sib_wait_send(self):
            for j in range(8):
                self.sib_copy(j).wait_send()

    half_q, half_t = QUERY_LEN // 2, BLOCK // 2
    g_qa = Gather(col_g, qa_ref, rows_of(qa, k, half_q), rows_of(qa, 1 - k, half_q), half_q, AG_A, SIB_A)
    g_qg = Gather(row_g, qg_ref, lanes_of(qg, k), lanes_of(qg, 1 - k), QUERY_LEN, AG_G, SIB_G)
    g_ta = Gather(row_g, ta_ref, whole(ta), None, BLOCK, AG_TA, None)
    g_tg = Gather(col_g, tg_ref, rows_of(tg, k, half_t), rows_of(tg, 1 - k, half_t), half_t, AG_TG, SIB_TG)
    queries, trains = (g_qa, g_qg), (g_ta, g_tg)

    copies = [
        pltpu.make_async_copy(eig_ref, rcp, local.at[0]),
        pltpu.make_async_copy(qa_ref, g_qa.full(g_qa.own), local.at[1]),
        pltpu.make_async_copy(qg_ref, g_qg.full(g_qg.own), local.at[2]),
        pltpu.make_async_copy(ab_ref, ab, local.at[3]),
        pltpu.make_async_copy(
            gb_ref.at[:, lanes(k)], gb.at[pl.ds(pl.multiple_of(k * TILE_J, TILE_J), TILE_J)], local.at[4]
        ),
        pltpu.make_async_copy(ta_ref, g_ta.full(g_ta.own), local.at[5]),
        pltpu.make_async_copy(tg_ref, g_tg.full(g_tg.own), local.at[6]),
    ]

    barrier = pltpu.get_barrier_semaphore()
    row_peers = [((r + d) % ROWS, c) for d in range(1, ROWS)]
    col_peers = [(r, (c + d) % COLS) for d in range(1, COLS)]
    for dev in row_peers + col_peers:
        pl.semaphore_signal(barrier, inc=1, device_id=dev, device_id_type=MESH)
    for cp in copies:
        cp.start()
    pl.semaphore_wait(barrier, ROWS + COLS - 2)

    for g in queries:
        g.start("pair")
    for g in queries:
        g.start("near0")
        g.sib_start(0)
    own_basis = gb.at[pl.ds(pl.multiple_of(k * TILE_J, TILE_J), TILE_J)]
    sib_basis = gb.at[pl.ds(pl.multiple_of((1 - k) * TILE_J, TILE_J), TILE_J)]
    basis_copy = remote(gb_ref.at[:, lanes(1 - k)], own_basis, SIB_BASIS, sib)
    basis_copy.start()
    for g in trains:
        g.start("near0")
    g_tg.sib_start(0)

    copies[0].wait()
    rcp[...] = 1.0 / (QUERY_LEN * (rcp[...] + DAMPING))

    for g in queries:
        g.wait("near0")
        g.start("far0")
        g.sib_start(2, 3)
    for g in queries:
        g.wait("pair")
        g.start("near1")
        g.sib_start(1)
    for g in trains:
        g.start("pair")
    for g in trains:
        g.wait("near0")
        g.start("far0")
    g_tg.sib_start(2, 3)
    for g in queries:
        g.wait("near1")
        g.start("far1")
        g.sib_start(4, 5)
    for g in queries:
        g.wait("far0")
        g.wait("far1")
        g.sib_start(6, 7)
    for g in queries:
        g.sib_wait()
    remote(sib_basis, sib_basis, SIB_BASIS, sib).wait_recv()
    for cp in copies[1:]:
        cp.wait()

    kinds = ((0, row_g), (1, col_g))

    def sem(t, ch, j):
        return REDUCE + (ch * 2 + t) * PER_REDUCE + j

    def rows(ch, v, lo=0, n=PIECE):
        return pl.ds(pl.multiple_of(ch * CHUNK_TOKENS + v * PIECE + lo, 16), n)

    def rotated(t, ds):
        if t == 0:
            return rot_a.at[ds]
        return rot_g.at[ds, lanes(k)]

    def at(g, d):
        return (g.u + d) % 4

    def reduce_copies(t, g, ch, step):
        if step == 1:
            v = at(g, 2)
            return [
                (part.at[t, rows(ch, v, 0, HALF)], near.at[t, ch, 0], sem(t, ch, 0), g.up),
                (part.at[t, rows(ch, v, HALF, HALF)], near.at[t, ch, 1], sem(t, ch, 1), g.dn),
            ]
        if step == 2:
            return [
                (part.at[t, rows(ch, at(g, 1))], mid.at[t, ch, 0], sem(t, ch, 2), g.up),
                (part.at[t, rows(ch, at(g, 3))], mid.at[t, ch, 1], sem(t, ch, 3), g.dn),
            ]
        if step == 3:
            return [(mine.at[t, ch], other.at[t, ch], sem(t, ch, 4), g.pair)]
        if step == 4:
            v = rotated(t, rows(ch, g.u))
            return [(v, v, sem(t, ch, 5), g.up), (v, v, sem(t, ch, 6), g.dn)]
        lo = rotated(t, rows(ch, at(g, 3), 0, HALF))
        hi = rotated(t, rows(ch, at(g, 1), HALF, HALF))
        return [(lo, lo, sem(t, ch, 7), g.up), (hi, hi, sem(t, ch, 8), g.dn)]

    def reduce_start(t, g, ch, step):
        for a in reduce_copies(t, g, ch, step):
            remote(*a).start()

    def landed(v, i, dev):
        remote(v, v, i, dev).wait_recv()

    def chunk_rows(ch):
        return pl.ds(pl.multiple_of(ch * CHUNK_TOKENS, 16), CHUNK_TOKENS)

    def sib_rot(ch):
        v = rot_g.at[chunk_rows(ch), lanes(k)]
        return remote(v, v, sem(1, ch, 9), sib)

    def partials(ch, carry):
        for i in range(PER_CHUNK):
            q = ch * PER_CHUNK + i
            ds = pl.ds(pl.multiple_of(q * QUERY_LEN, QUERY_LEN), QUERY_LEN)
            part[0, ds] = jnp.dot(qa[q], ab[...], preferred_element_type=F32).astype(BF16)
            part[1, ds] = jnp.dot(qg[q], gb[...], preferred_element_type=F32).astype(BF16)
        for t, g in kinds:
            reduce_start(t, g, ch, 1)
        return carry

    lax.fori_loop(0, CHUNKS, partials, 0)

    for g in trains:
        g.wait("pair")
        g.start("near1")
    g_tg.sib_start(1)

    def step2(ch):
        for t, g in kinds:
            landed(near.at[t, ch, 0], sem(t, ch, 0), g.dn)
            ds = rows(ch, at(g, 1), 0, HALF)
            part[t, ds] = (part[t, ds].astype(F32) + near[t, ch, 0].astype(F32)).astype(BF16)
            landed(near.at[t, ch, 1], sem(t, ch, 1), g.up)
            ds = rows(ch, at(g, 3), HALF, HALF)
            part[t, ds] = (part[t, ds].astype(F32) + near[t, ch, 1].astype(F32)).astype(BF16)
            reduce_start(t, g, ch, 2)

    def step3(ch):
        for t, g in kinds:
            landed(mid.at[t, ch, 0], sem(t, ch, 2), g.dn)
            landed(mid.at[t, ch, 1], sem(t, ch, 3), g.up)
            total = part[t, rows(ch, g.u)].astype(F32) + mid[t, ch, 0].astype(F32) + mid[t, ch, 1].astype(F32)
            mine[t, ch] = total.astype(BF16)
            reduce_start(t, g, ch, 3)

    def step4(ch):
        for t, g in kinds:
            landed(other.at[t, ch], sem(t, ch, 4), g.pair)
            total = (mine[t, ch].astype(F32) + other[t, ch].astype(F32)).astype(BF16)
            if t == 0:
                rot_a[rows(ch, g.u)] = total
            else:
                rot_g[rows(ch, g.u), lanes(k)] = total
            reduce_start(t, g, ch, 4)

    def step5(ch):
        for t, g in kinds:
            landed(rotated(t, rows(ch, at(g, 3))), sem(t, ch, 5), g.dn)
            landed(rotated(t, rows(ch, at(g, 1))), sem(t, ch, 6), g.up)
            reduce_start(t, g, ch, 5)

    def step6(ch):
        for t, g in reversed(kinds):
            landed(rotated(t, rows(ch, at(g, 2), 0, HALF)), sem(t, ch, 7), g.dn)
            landed(rotated(t, rows(ch, at(g, 2), HALF, HALF)), sem(t, ch, 8), g.up)
            if t == 1:
                sib_rot(ch).start()

    def make_panels(ch):
        v = rot_g.at[chunk_rows(ch), lanes(1 - k)]
        landed(v, sem(1, ch, 9), sib)
        for i in range(PER_CHUNK):
            ds = pl.ds(pl.multiple_of((ch * PER_CHUNK + i) * QUERY_LEN, QUERY_LEN), QUERY_LEN)
            outer = lax.dot_general(
                rot_g[ds], rot_a[ds], (((0,), (0,)), ((), ())), preferred_element_type=F32
            )
            panels[:, pl.ds(i * TILE_J, TILE_J)] = (outer * rcp[...]).astype(BF16)

    def score(ch, lo, hi):
        q_of = lax.broadcasted_iota(jnp.int32, (QUERIES, PER_CHUNK * 128), 0)
        lane = lax.broadcasted_iota(jnp.int32, (QUERIES, PER_CHUNK * 128), 1)
        pick = jnp.where(q_of == ch * PER_CHUNK + lane // 128, 1.0, 0.0).astype(BF16)

        def tile(tt, carry):
            mapped = jnp.dot(tg[tt], panels[...], preferred_element_type=F32)
            acts = ta[tt].astype(F32)
            sums = []
            for i in range(PER_CHUNK):
                total = None
                for j in range(TILE_J // 128):
                    term = mapped[:, i * TILE_J + j * 128 : i * TILE_J + (j + 1) * 128] * acts[:, j * 128 : (j + 1) * 128]
                    total = term if total is None else total + term
                sums.append(total.astype(BF16))
            lanes_sum = sums[0] if PER_CHUNK == 1 else jnp.concatenate(sums, axis=1)
            acc[tt] += lax.dot_general(
                pick, lanes_sum, (((1,), (1,)), ((), ())), preferred_element_type=F32
            )
            return carry

        lax.fori_loop(lo, hi, tile, 0)

    acc[...] = jnp.zeros_like(acc)

    def group(i, carry):
        def when(ch, f):
            @pl.when((ch >= 0) & (ch < CHUNKS))
            def _():
                f(ch)

        when(i - 1, step5)
        when(i, step2)
        when(i - 2, lambda ch: score(ch, 0, 4))
        when(i - 1, step6)
        when(i, step3)
        when(i - 2, lambda ch: score(ch, 4, 8))
        when(i, step4)

        @pl.when(i == 0)
        def _():
            for g in trains:
                g.wait("near1")
                g.start("far1")
            g_tg.sib_start(4, 5)

        @pl.when(i == 1)
        def _():
            for g in trains:
                g.wait("far0")
                g.wait("far1")
            g_tg.sib_start(6, 7)
            g_tg.sib_wait()

        when(i - 1, make_panels)
        return carry

    lax.fori_loop(0, CHUNKS + 2, group, 0)

    def to_row(d):
        peer = (r + d) % ROWS
        return remote(acc.at[peer], first.at[d - 1], FIRST + d - 1, (peer, c))

    for d in range(1, ROWS):
        to_row(d).start()
    total = acc[r]
    for d in range(1, ROWS):
        landed(first.at[d - 1], FIRST + d - 1, ((r + ROWS - d) % ROWS, c))
        total = total + first[d - 1]
    total = total / D
    for j in range(COLS):
        split[j] = total[:, j * OWNED : (j + 1) * OWNED]

    def to_col(d):
        peer = (c + d) % COLS
        return remote(split.at[peer], second.at[d - 1], SECOND + d - 1, (r, peer))

    for d in range(1, COLS):
        to_col(d).start()
    total = split[c]
    for d in range(1, COLS):
        landed(second.at[d - 1], SECOND + d - 1, (r, (c + COLS - d) % COLS))
        total = total + second[d - 1]
    out_ref[...] = total

    for g in queries + trains:
        g.wait_send()
    for g in (g_qa, g_qg, g_tg):
        g.sib_wait_send()
    basis_copy.wait_send()

    def drain(ch, carry):
        for t, g in kinds:
            for step in range(1, 6):
                for a in reduce_copies(t, g, ch, step):
                    remote(*a).wait_send()
        sib_rot(ch).wait_send()
        return carry

    lax.fori_loop(0, CHUNKS, drain, 0)
    for d in range(1, ROWS):
        to_row(d).wait_send()
    for d in range(1, COLS):
        to_col(d).wait_send()


def shards(*args):
    any_spec = pl.BlockSpec(memory_space=pl.ANY)
    vmem = pltpu.VMEM
    return pl.pallas_call(
        kernel,
        out_shape=jax.ShapeDtypeStruct((QUERIES, OWNED), F32),
        in_specs=[any_spec] * 7,
        out_specs=pl.BlockSpec(memory_space=pltpu.VMEM),
        scratch_shapes=[
            vmem((8, QUERY_LEN, TILE_I), BF16),
            vmem((8, QUERY_LEN, 2 * TILE_J), BF16),
            vmem((TILE_I, TILE_J), BF16),
            vmem((2 * TILE_J, TILE_J), BF16),
            vmem((TILE_I, TILE_J), F32),
            vmem((8, BLOCK, TILE_J), BF16),
            vmem((8, BLOCK, TILE_I), BF16),
            vmem((2, TOKENS, TILE_J), BF16),
            vmem((TOKENS, TILE_J), BF16),
            vmem((TOKENS, TILE_I), BF16),
            vmem((2, CHUNKS, 2, HALF, TILE_J), BF16),
            vmem((2, CHUNKS, 2, PIECE, TILE_J), BF16),
            vmem((2, CHUNKS, PIECE, TILE_J), BF16),
            vmem((2, CHUNKS, PIECE, TILE_J), BF16),
            vmem((TILE_I, PER_CHUNK * TILE_J), BF16),
            vmem((8, QUERIES, BLOCK), F32),
            vmem((ROWS - 1, QUERIES, BLOCK), F32),
            vmem((COLS, QUERIES, OWNED), F32),
            vmem((COLS - 1, QUERIES, OWNED), F32),
            pltpu.SemaphoreType.DMA((7,)),
            pltpu.SemaphoreType.DMA((N_SEMS,)),
            pltpu.SemaphoreType.DMA((N_SEMS,)),
        ],
        compiler_params=pltpu.CompilerParams(
            collective_id=0, has_side_effects=True, vmem_limit_bytes=50 * 1024 * 1024
        ),
        name="influence",
    )(*args)


def solution(mesh):
    return jax.shard_map(
        shards,
        mesh=mesh,
        in_specs=(
            P("col", "row"),
            P("row", "col"),
            P("row", "col"),
            P("col", "row"),
            P("row", "col"),
            P("row", "col"),
            P("col", "row"),
        ),
        out_specs=P(None, ("row", "col")),
        check_vma=False,
    )
```

time: 467 us -> 136 us (0.29)
  blocking collectives: 200 us -> 0 us
  waiting for transfers between devices: 182 us -> 0 us
  Pallas kernels: 0 us -> 128 us
  matrix products: 58.2 us -> 0 us
  between operations: 13.2 us -> 0.02 us
    psum x2 -> x0, blocking collectives: 200 us -> none  [the longest x1 111 us: shards(): rot_grads = lax.psum(grads_part, 'col').astype(jnp.bfloat16)]
    unnamed x6 -> x0, waiting for transfers between devices: 146 us -> none
    pallas_call x0 -> x1, Pallas kernels: none -> 128 us  [shards(): pl.pallas_call(kernel, out_shape=jax.ShapeDtypeStruct((QUERIES, OWNED), F...]
    dot_general x11 -> x0, matrix products: 58.2 us -> none  [the longest x8 41.1 us: per_query(): lax.dot_general(act_rows, panel, (((1,), (1,)), ((), ())), preferred_elem...]
    all_gather x4 -> x0, waiting for transfers between devices: 35.8 us -> none  [the longest x1 35.8 us: shards(): grads_in = lax.all_gather(query_grads, 'row', axis=0, tiled=True)]
    unnamed x5 -> x15, local copies, waits for them, and re-layouts: 1.37 us -> 7.73 us
    while x1 -> x0, local copies, waits for them, and re-layouts: 6.34 us -> none  [tile_scores(): return lax.map(per_query, panels)]
  transfers between devices with their start and end apart: 5 -> 0, of which waited for: 2 -> 0; matrix products, arithmetic and copies ran while one was open for 5% -> 0% of each run, Pallas kernels for 0% -> 0%
where the time goes in v1:
time: 136 us
  Pallas kernels  128 us (94%)
  local copies, waits for them, and re-layouts  7.73 us (6%)
    pallas_call x1, Pallas kernels, shards(): pl.pallas_call(kernel, out_shape=jax.ShapeDtypeStruct((QUERIES, OWNED), F...  128 us
    unnamed x15, local copies, waits for them, and re-layouts  7.73 us

profile of v1, /device:TPU:1, one launch (start us, length us, event | category | flops | bytes accessed | tf_op | source)
XLA Modules:
  0.0 136.1 jit_solution(8233665321406802838)
XLA Ops:
  0.0 0.0 copy-start
  0.0 1.3 copy-done
  1.3 0.0 copy-start.1
  1.3 1.1 copy-done.1
  2.3 0.0 copy-start.2
  2.3 1.1 copy-done.2
  3.4 0.0 copy-start.3
  3.4 0.9 copy-done.3
  4.3 0.0 copy-start.4
  4.3 0.9 copy-done.4
  5.3 0.0 copy-start.5
  5.3 0.9 copy-done.5
  6.2 0.0 copy-start.6
  6.2 0.9 copy-done.6
  7.1 128.4 %influence.1 = f32[8,20]{1,0:T(8,128)S(1)} custom-call(bf16[128,768]{1,0:T(8,128)(2,1)S(1)} %copy-done.5, bf16[256,384]{1,0:T(8,128)(2,1)S(1)} %copy-done.6, bf16[768,384]{1,0:T(8,128)(2,1)S(1)} %copy-done.1, bf16[384,768]{1,0:T(8,128)(2,1)S(1)} %copy-done.2, f32[768,384]{1,0:T(8,128)S(1)} %copy-done, bf16[320,384]{1,0:T(8,128)(2,1)S(1)} %copy-done.3, ...), custom_call_target="tpu_custom_call" | custom-call | tf_op jit(solution)/shard_map/influence/pallas_call | solution.py:477
  135.5 0.6 copy.9
Async XLA Ops:
  0.0 1.3 copy-start
  1.3 1.1 copy-start.1
  2.3 1.1 copy-start.2
  3.4 0.9 copy-start.3
  4.3 0.9 copy-start.4
  5.3 0.9 copy-start.5
  6.2 0.9 copy-start.6

commit v2 on v1

--- a/solution.py
+++ b/solution.py
@@ -25,6 +25,9 @@
 PIECE = CHUNK_TOKENS // 4
 HALF = PIECE // 2
 
+EVERY = 1
+LAST = 4
+
 MESH = pl.DeviceIdType.MESH
 BF16 = jnp.bfloat16
 F32 = jnp.float32
@@ -42,7 +45,7 @@
 def kernel(
     qa_ref, qg_ref, ab_ref, gb_ref, eig_ref, ta_ref, tg_ref, out_ref,
     qa, qg, ab, gb, rcp, ta, tg, part, rot_a, rot_g, near, mid, mine, other,
-    panels, acc, first, split, second, local, sent, got,
+    panels, acc, blocks, first, split, second, local, sent, got,
 ):
     r = lax.axis_index("row")
     c = lax.axis_index("col")
@@ -202,6 +205,12 @@
         cp.start()
     pl.semaphore_wait(barrier, ROWS + COLS - 2)
 
+    def train_near0():
+        for g in trains:
+            g.wait("near0")
+            g.start("far0")
+        g_tg.sib_start(2, 3)
+
     for g in queries:
         g.start("pair")
     for g in queries:
@@ -228,10 +237,7 @@
         g.sib_start(1)
     for g in trains:
         g.start("pair")
-    for g in trains:
-        g.wait("near0")
-        g.start("far0")
-    g_tg.sib_start(2, 3)
+    train_near0()
     for g in queries:
         g.wait("near1")
         g.start("far1")
@@ -297,22 +303,15 @@
         v = rot_g.at[chunk_rows(ch), lanes(k)]
         return remote(v, v, sem(1, ch, 9), sib)
 
-    def partials(ch, carry):
-        for i in range(PER_CHUNK):
-            q = ch * PER_CHUNK + i
-            ds = pl.ds(pl.multiple_of(q * QUERY_LEN, QUERY_LEN), QUERY_LEN)
-            part[0, ds] = jnp.dot(qa[q], ab[...], preferred_element_type=F32).astype(BF16)
-            part[1, ds] = jnp.dot(qg[q], gb[...], preferred_element_type=F32).astype(BF16)
+    def partials(ch):
+        ds = chunk_rows(ch)
+        of = pl.ds(ch * PER_CHUNK, PER_CHUNK)
+        for t, ref, basis in ((0, qa, ab), (1, qg, gb)):
+            part[t, ds] = jnp.dot(
+                ref[of].reshape(CHUNK_TOKENS, TILE_I), basis[...], preferred_element_type=F32
+            ).astype(BF16)
         for t, g in kinds:
             reduce_start(t, g, ch, 1)
-        return carry
-
-    lax.fori_loop(0, CHUNKS, partials, 0)
-
-    for g in trains:
-        g.wait("pair")
-        g.start("near1")
-    g_tg.sib_start(1)
 
     def step2(ch):
         for t, g in kinds:
@@ -363,74 +362,87 @@
             outer = lax.dot_general(
                 rot_g[ds], rot_a[ds], (((0,), (0,)), ((), ())), preferred_element_type=F32
             )
-            panels[:, pl.ds(i * TILE_J, TILE_J)] = (outer * rcp[...]).astype(BF16)
-
-    def score(ch, lo, hi):
+            panels[ch % 2, :, pl.ds(i * TILE_J, TILE_J)] = (outer * rcp[...]).astype(BF16)
+
+    def score(ch, h):
         q_of = lax.broadcasted_iota(jnp.int32, (QUERIES, PER_CHUNK * 128), 0)
         lane = lax.broadcasted_iota(jnp.int32, (QUERIES, PER_CHUNK * 128), 1)
         pick = jnp.where(q_of == ch * PER_CHUNK + lane // 128, 1.0, 0.0).astype(BF16)
 
-        def tile(tt, carry):
-            mapped = jnp.dot(tg[tt], panels[...], preferred_element_type=F32)
-            acts = ta[tt].astype(F32)
-            sums = []
-            for i in range(PER_CHUNK):
-                total = None
-                for j in range(TILE_J // 128):
-                    term = mapped[:, i * TILE_J + j * 128 : i * TILE_J + (j + 1) * 128] * acts[:, j * 128 : (j + 1) * 128]
-                    total = term if total is None else total + term
-                sums.append(total.astype(BF16))
-            lanes_sum = sums[0] if PER_CHUNK == 1 else jnp.concatenate(sums, axis=1)
-            acc[tt] += lax.dot_general(
-                pick, lanes_sum, (((1,), (1,)), ((), ())), preferred_element_type=F32
-            )
-            return carry
-
-        lax.fori_loop(lo, hi, tile, 0)
+        mapped = jnp.dot(
+            tg[pl.ds(4 * h, 4)].reshape(4 * BLOCK, TILE_I), panels[ch % 2], preferred_element_type=F32
+        )
+        acts = ta[pl.ds(4 * h, 4)].reshape(4 * BLOCK, TILE_J).astype(F32)
+        sums = []
+        for i in range(PER_CHUNK):
+            total = None
+            for j in range(TILE_J // 128):
+                term = mapped[:, i * TILE_J + j * 128 : i * TILE_J + (j + 1) * 128] * acts[:, j * 128 : (j + 1) * 128]
+                total = term if total is None else total + term
+            sums.append(total.astype(BF16))
+        lanes_sum = sums[0] if PER_CHUNK == 1 else jnp.concatenate(sums, axis=1)
+        acc[h] += lax.dot_general(
+            pick, lanes_sum, (((1,), (1,)), ((), ())), preferred_element_type=F32
+        )
 
     acc[...] = jnp.zeros_like(acc)
 
-    def group(i, carry):
-        def when(ch, f):
-            @pl.when((ch >= 0) & (ch < CHUNKS))
+    def slot(w, carry):
+        def when(step, f):
+            ch = (w - step) // EVERY
+
+            @pl.when((w >= step) & (w - step == ch * EVERY) & (ch < CHUNKS))
             def _():
                 f(ch)
 
-        when(i - 1, step5)
-        when(i, step2)
-        when(i - 2, lambda ch: score(ch, 0, 4))
-        when(i - 1, step6)
-        when(i, step3)
-        when(i - 2, lambda ch: score(ch, 4, 8))
-        when(i, step4)
-
-        @pl.when(i == 0)
-        def _():
-            for g in trains:
-                g.wait("near1")
-                g.start("far1")
-            g_tg.sib_start(4, 5)
-
-        @pl.when(i == 1)
-        def _():
-            for g in trains:
-                g.wait("far0")
-                g.wait("far1")
-            g_tg.sib_start(6, 7)
-            g_tg.sib_wait()
-
-        when(i - 1, make_panels)
+        def at_slot(n, f):
+            pl.when(w == n)(f)
+
+        when(4, make_panels)
+        when(0, partials)
+        at_slot(0, train_pair)
+        when(3, step5)
+        at_slot(1, train_near1)
+        at_slot(2, train_far)
+        at_slot(4, g_tg.sib_wait)
+        when(4, lambda ch: score(ch, 0))
+        when(1, step3)
+        when(2, step4)
+        when(4, lambda ch: score(ch, 1))
+        when(0, step2)
+        when(3, step6)
         return carry
 
-    lax.fori_loop(0, CHUNKS + 2, group, 0)
+    def train_pair():
+        for g in trains:
+            g.wait("pair")
+            g.start("near1")
+        g_tg.sib_start(1)
+
+    def train_near1():
+        for g in trains:
+            g.wait("near1")
+            g.start("far1")
+        g_tg.sib_start(4, 5)
+
+    def train_far():
+        for g in trains:
+            g.wait("far0")
+            g.wait("far1")
+        g_tg.sib_start(6, 7)
+
+    lax.fori_loop(0, (CHUNKS - 1) * EVERY + LAST + 1, slot, 0)
+
+    for j in range(ROWS):
+        blocks[j] = acc[j // 4, :, (j % 4) * BLOCK : (j % 4 + 1) * BLOCK]
 
     def to_row(d):
         peer = (r + d) % ROWS
-        return remote(acc.at[peer], first.at[d - 1], FIRST + d - 1, (peer, c))
+        return remote(blocks.at[peer], first.at[d - 1], FIRST + d - 1, (peer, c))
 
     for d in range(1, ROWS):
         to_row(d).start()
-    total = acc[r]
+    total = blocks[r]
     for d in range(1, ROWS):
         landed(first.at[d - 1], FIRST + d - 1, ((r + ROWS - d) % ROWS, c))
         total = total + first[d - 1]
@@ -494,8 +506,9 @@
             vmem((2, CHUNKS, 2, PIECE, TILE_J), BF16),
             vmem((2, CHUNKS, PIECE, TILE_J), BF16),
             vmem((2, CHUNKS, PIECE, TILE_J), BF16),
-            vmem((TILE_I, PER_CHUNK * TILE_J), BF16),
-            vmem((8, QUERIES, BLOCK), F32),
+            vmem((2, TILE_I, PER_CHUNK * TILE_J), BF16),
+            vmem((2, QUERIES, 4 * BLOCK), F32),
+            vmem((ROWS, QUERIES, BLOCK), F32),
             vmem((ROWS - 1, QUERIES, BLOCK), F32),
             vmem((COLS, QUERIES, OWNED), F32),
             vmem((COLS - 1, QUERIES, OWNED), F32),
@@ -504,7 +517,7 @@
             pltpu.SemaphoreType.DMA((N_SEMS,)),
         ],
         compiler_params=pltpu.CompilerParams(
-            collective_id=0, has_side_effects=True, vmem_limit_bytes=50 * 1024 * 1024
+            collective_id=0, has_side_effects=True, vmem_limit_bytes=62 * 1024 * 1024
         ),
         name="influence",
     )(*args)

time: 136 us -> 103 us (0.76)
  Pallas kernels: 128 us -> 101 us
  local copies, waits for them, and re-layouts: 7.73 us -> 1.28 us
    pallas_call x1, Pallas kernels: 128 us -> 101 us  [shards(): pl.pallas_call(kernel, out_shape=jax.ShapeDtypeStruct((QUERIES, OWNED), F...]
    unnamed x15 -> x1, local copies, waits for them, and re-layouts: 7.73 us -> 1.28 us
where the time goes in v2:
time: 103 us; the launch traced here: 102 us
  Pallas kernels  101 us (98%)
  local copies, waits for them, and re-layouts  1.28 us (1%)
    pallas_call x1, Pallas kernels, shards(): pl.pallas_call(kernel, out_shape=jax.ShapeDtypeStruct((QUERIES, OWNED), F...  101 us

profile of v2, /device:TPU:1, one launch (start us, length us, event | category | flops | bytes accessed | tf_op | source)
XLA Modules:
  0.0 102.5 jit_solution(10759555043089035153)
XLA Ops:
  0.0 101.2 %influence.1 = f32[8,20]{1,0:T(8,128)} custom-call(bf16[128,768]{1,0:T(8,128)(2,1)} %qa_ref.1, bf16[256,384]{1,0:T(8,128)(2,1)} %qg_ref.1, bf16[768,384]{1,0:T(8,128)(2,1)} %ab_ref.1, bf16[384,768]{1,0:T(8,128)(2,1)} %gb_ref.1, f32[768,384]{1,0:T(8,128)} %eig_ref.1, bf16[320,384]{1,0:T(8,128)(2,1)} %ta_ref.1, bf16[160,768]{1,0:T(8,128)(2,1)} %tg_ref.1), custom_call_target="tpu_custom_call" | custom-call | tf_op jit(solution)/shard_map/influence/pallas_call | solution.py:489
  101.2 1.3 %copy.9 = f32[8,20]{1,0:T(8,128)} copy(f32[8,20]{1,0:T(8,128)} %influence.1) | data formatting | bytes 1280

commit v3 on v2

--- a/solution.py
+++ b/solution.py
@@ -25,8 +25,9 @@
 PIECE = CHUNK_TOKENS // 4
 HALF = PIECE // 2
 
-EVERY = 1
-LAST = 4
+ORDER = (
+    "q0", "q1", "t0", "tp", "qn1", "qf0", "qf1", "tn1", "qe", "P0", "P1", "P3", "20", "21", "P2", "30", "tf1", "22", "31", "23", "40", "32", "tf0", "50", "41", "33", "42", "60", "te", "51", "N0", "tw", "S0", "52", "43", "61", "T0", "N1", "62", "S1", "53", "T1", "N2", "S2", "63", "T2", "N3", "S3", "T3",
+)
 
 MESH = pl.DeviceIdType.MESH
 BF16 = jnp.bfloat16
@@ -205,52 +206,65 @@
         cp.start()
     pl.semaphore_wait(barrier, ROWS + COLS - 2)
 
+    own_basis = gb.at[pl.ds(pl.multiple_of(k * TILE_J, TILE_J), TILE_J)]
+    sib_basis = gb.at[pl.ds(pl.multiple_of((1 - k) * TILE_J, TILE_J), TILE_J)]
+    basis_copy = remote(gb_ref.at[:, lanes(1 - k)], own_basis, SIB_BASIS, sib)
+
+    def query_pair():
+        for g in queries:
+            g.start("pair")
+
+    def query_own():
+        for g in queries:
+            g.start("near0")
+            g.sib_start(0)
+        basis_copy.start()
+
+    def train_own():
+        for g in trains:
+            g.start("near0")
+        g_tg.sib_start(0)
+        copies[0].wait()
+        rcp[...] = 1.0 / (QUERY_LEN * (rcp[...] + DAMPING))
+
+    def query_near0():
+        for g in queries:
+            g.wait("near0")
+            g.start("far0")
+            g.sib_start(2, 3)
+
+    def query_pair_in():
+        for g in queries:
+            g.wait("pair")
+            g.start("near1")
+            g.sib_start(1)
+
+    def train_pair_out():
+        for g in trains:
+            g.start("pair")
+
     def train_near0():
         for g in trains:
             g.wait("near0")
             g.start("far0")
         g_tg.sib_start(2, 3)
 
-    for g in queries:
-        g.start("pair")
-    for g in queries:
-        g.start("near0")
-        g.sib_start(0)
-    own_basis = gb.at[pl.ds(pl.multiple_of(k * TILE_J, TILE_J), TILE_J)]
-    sib_basis = gb.at[pl.ds(pl.multiple_of((1 - k) * TILE_J, TILE_J), TILE_J)]
-    basis_copy = remote(gb_ref.at[:, lanes(1 - k)], own_basis, SIB_BASIS, sib)
-    basis_copy.start()
-    for g in trains:
-        g.start("near0")
-    g_tg.sib_start(0)
-
-    copies[0].wait()
-    rcp[...] = 1.0 / (QUERY_LEN * (rcp[...] + DAMPING))
-
-    for g in queries:
-        g.wait("near0")
-        g.start("far0")
-        g.sib_start(2, 3)
-    for g in queries:
-        g.wait("pair")
-        g.start("near1")
-        g.sib_start(1)
-    for g in trains:
-        g.start("pair")
-    train_near0()
-    for g in queries:
-        g.wait("near1")
-        g.start("far1")
-        g.sib_start(4, 5)
-    for g in queries:
-        g.wait("far0")
-        g.wait("far1")
-        g.sib_start(6, 7)
-    for g in queries:
-        g.sib_wait()
-    remote(sib_basis, sib_basis, SIB_BASIS, sib).wait_recv()
-    for cp in copies[1:]:
-        cp.wait()
+    def query_near1():
+        for g in queries:
+            g.wait("near1")
+            g.start("far1")
+            g.sib_start(4, 5)
+
+    def query_far():
+        for g in queries:
+            g.wait("far0")
+            g.wait("far1")
+            g.sib_start(6, 7)
+        for g in queries:
+            g.sib_wait()
+        remote(sib_basis, sib_basis, SIB_BASIS, sib).wait_recv()
+        for cp in copies[1:]:
+            cp.wait()
 
     kinds = ((0, row_g), (1, col_g))
 
@@ -365,53 +379,20 @@
             panels[ch % 2, :, pl.ds(i * TILE_J, TILE_J)] = (outer * rcp[...]).astype(BF16)
 
     def score(ch, h):
-        q_of = lax.broadcasted_iota(jnp.int32, (QUERIES, PER_CHUNK * 128), 0)
-        lane = lax.broadcasted_iota(jnp.int32, (QUERIES, PER_CHUNK * 128), 1)
-        pick = jnp.where(q_of == ch * PER_CHUNK + lane // 128, 1.0, 0.0).astype(BF16)
-
         mapped = jnp.dot(
             tg[pl.ds(4 * h, 4)].reshape(4 * BLOCK, TILE_I), panels[ch % 2], preferred_element_type=F32
         )
         acts = ta[pl.ds(4 * h, 4)].reshape(4 * BLOCK, TILE_J).astype(F32)
-        sums = []
         for i in range(PER_CHUNK):
+            q = ch * PER_CHUNK + i
             total = None
             for j in range(TILE_J // 128):
                 term = mapped[:, i * TILE_J + j * 128 : i * TILE_J + (j + 1) * 128] * acts[:, j * 128 : (j + 1) * 128]
                 total = term if total is None else total + term
-            sums.append(total.astype(BF16))
-        lanes_sum = sums[0] if PER_CHUNK == 1 else jnp.concatenate(sums, axis=1)
-        acc[h] += lax.dot_general(
-            pick, lanes_sum, (((1,), (1,)), ((), ())), preferred_element_type=F32
-        )
+            acc[h, :, q : q + 1] = jnp.sum(total, axis=1, keepdims=True)
 
     acc[...] = jnp.zeros_like(acc)
-
-    def slot(w, carry):
-        def when(step, f):
-            ch = (w - step) // EVERY
-
-            @pl.when((w >= step) & (w - step == ch * EVERY) & (ch < CHUNKS))
-            def _():
-                f(ch)
-
-        def at_slot(n, f):
-            pl.when(w == n)(f)
-
-        when(4, make_panels)
-        when(0, partials)
-        at_slot(0, train_pair)
-        when(3, step5)
-        at_slot(1, train_near1)
-        at_slot(2, train_far)
-        at_slot(4, g_tg.sib_wait)
-        when(4, lambda ch: score(ch, 0))
-        when(1, step3)
-        when(2, step4)
-        when(4, lambda ch: score(ch, 1))
-        when(0, step2)
-        when(3, step6)
-        return carry
+    split[...] = jnp.zeros_like(split)
 
     def train_pair():
         for g in trains:
@@ -431,10 +412,28 @@
             g.wait("far1")
         g_tg.sib_start(6, 7)
 
-    lax.fori_loop(0, (CHUNKS - 1) * EVERY + LAST + 1, slot, 0)
-
-    for j in range(ROWS):
-        blocks[j] = acc[j // 4, :, (j % 4) * BLOCK : (j % 4 + 1) * BLOCK]
+    def train_end():
+        g_tg.sib_wait()
+
+    events = {
+        "q0": query_pair, "q1": query_own, "t0": train_own, "qf0": query_near0, "qn1": query_pair_in,
+        "tp": train_pair_out, "tf0": train_near0, "qf1": query_near1, "qe": query_far,
+        "tn1": train_pair, "tf1": train_near1, "te": train_far, "tw": train_end,
+    }
+    steps = {
+        "P": partials, "2": step2, "3": step3, "4": step4, "5": step5, "6": step6,
+        "N": make_panels, "S": lambda ch: score(ch, 0), "T": lambda ch: score(ch, 1),
+    }
+    for name in ORDER:
+        if name in events:
+            events[name]()
+        else:
+            steps[name[0]](int(name[1:]))
+
+    for h in range(2):
+        turned = acc[h].T[:QUERIES]
+        for j in range(4):
+            blocks[4 * h + j] = turned[:, j * BLOCK : (j + 1) * BLOCK]
 
     def to_row(d):
         peer = (r + d) % ROWS
@@ -448,7 +447,7 @@
         total = total + first[d - 1]
     total = total / D
     for j in range(COLS):
-        split[j] = total[:, j * OWNED : (j + 1) * OWNED]
+        split[j, :, :OWNED] = total[:, j * OWNED : (j + 1) * OWNED]
 
     def to_col(d):
         peer = (c + d) % COLS
@@ -460,7 +459,7 @@
     for d in range(1, COLS):
         landed(second.at[d - 1], SECOND + d - 1, (r, (c + COLS - d) % COLS))
         total = total + second[d - 1]
-    out_ref[...] = total
+    out_ref[...] = total[:, :OWNED]
 
     for g in queries + trains:
         g.wait_send()
@@ -507,11 +506,11 @@
             vmem((2, CHUNKS, PIECE, TILE_J), BF16),
             vmem((2, CHUNKS, PIECE, TILE_J), BF16),
             vmem((2, TILE_I, PER_CHUNK * TILE_J), BF16),
-            vmem((2, QUERIES, 4 * BLOCK), F32),
+            vmem((2, 4 * BLOCK, 128), F32),
             vmem((ROWS, QUERIES, BLOCK), F32),
             vmem((ROWS - 1, QUERIES, BLOCK), F32),
-            vmem((COLS, QUERIES, OWNED), F32),
-            vmem((COLS - 1, QUERIES, OWNED), F32),
+            vmem((COLS, QUERIES, 128), F32),
+            vmem((COLS - 1, QUERIES, 128), F32),
             pltpu.SemaphoreType.DMA((7,)),
             pltpu.SemaphoreType.DMA((N_SEMS,)),
             pltpu.SemaphoreType.DMA((N_SEMS,)),

time: 103 us -> 97.6 us (0.948)
  Pallas kernels: 101 us -> 96.2 us
    pallas_call x1, Pallas kernels: 101 us -> 96.2 us  [shards(): pl.pallas_call(kernel, out_shape=jax.ShapeDtypeStruct((QUERIES, OWNED), F...]
where the time goes in v3:
time: 97.6 us; the launch traced here: 97.5 us
  Pallas kernels  96.2 us (99%)
  local copies, waits for them, and re-layouts  1.28 us (1%)
    pallas_call x1, Pallas kernels, shards(): pl.pallas_call(kernel, out_shape=jax.ShapeDtypeStruct((QUERIES, OWNED), F...  96.2 us

profile of v3, /device:TPU:1, one launch (start us, length us, event | category | flops | bytes accessed | tf_op | source)
XLA Modules:
  0.0 97.5 jit_solution(4184862882650489456)
XLA Ops:
  0.0 96.2 %influence.1 = f32[8,20]{1,0:T(8,128)} custom-call(bf16[128,768]{1,0:T(8,128)(2,1)} %qa_ref.1, bf16[256,384]{1,0:T(8,128)(2,1)} %qg_ref.1, bf16[768,384]{1,0:T(8,128)(2,1)} %ab_ref.1, bf16[384,768]{1,0:T(8,128)(2,1)} %gb_ref.1, f32[768,384]{1,0:T(8,128)} %eig_ref.1, bf16[320,384]{1,0:T(8,128)(2,1)} %ta_ref.1, bf16[160,768]{1,0:T(8,128)(2,1)} %tg_ref.1), custom_call_target="tpu_custom_call" | custom-call | tf_op jit(solution)/shard_map/influence/pallas_call | solution.py:488
  96.2 1.3 %copy.9 = f32[8,20]{1,0:T(8,128)} copy(f32[8,20]{1,0:T(8,128)} %influence.1) | data formatting | bytes 1280

commit v4 on v3

--- a/solution.py
+++ b/solution.py
@@ -19,14 +19,15 @@
 BLOCK = TRAIN // 8
 OWNED = TRAIN // (ROWS * COLS)
 
-CHUNKS = 4
-PER_CHUNK = QUERIES // CHUNKS
-CHUNK_TOKENS = PER_CHUNK * QUERY_LEN
-PIECE = CHUNK_TOKENS // 4
-HALF = PIECE // 2
+SIZES = (2, 2, 2, 2)
+CHUNKS = len(SIZES)
+STARTS = tuple(sum(SIZES[:ch]) for ch in range(CHUNKS))
 
 ORDER = (
-    "q0", "q1", "t0", "tp", "qn1", "qf0", "qf1", "tn1", "qe", "P0", "P1", "P3", "20", "21", "P2", "30", "tf1", "22", "31", "23", "40", "32", "tf0", "50", "41", "33", "42", "60", "te", "51", "N0", "tw", "S0", "52", "43", "61", "T0", "N1", "62", "S1", "53", "T1", "N2", "S2", "63", "T2", "N3", "S3", "T3",
+    "q0", "q1", "t0", "qf0", "tp", "qn1", "tf0", "qf1", "tn1", "qe", "qw", "P0", "P1", "P2",
+    "20", "P3", "21", "22", "30", "23", "31", "32", "40", "tf1", "33", "50", "41", "te",
+    "42", "60", "51", "N0", "43", "tw", "S0", "52", "61", "T0", "N1", "53", "S1", "62",
+    "T1", "63", "N2", "S2", "T2", "N3", "S3", "T3",
 )
 
 MESH = pl.DeviceIdType.MESH
@@ -260,6 +261,8 @@
             g.wait("far0")
             g.wait("far1")
             g.sib_start(6, 7)
+
+    def query_end():
         for g in queries:
             g.sib_wait()
         remote(sib_basis, sib_basis, SIB_BASIS, sib).wait_recv()
@@ -271,8 +274,22 @@
     def sem(t, ch, j):
         return REDUCE + (ch * 2 + t) * PER_REDUCE + j
 
-    def rows(ch, v, lo=0, n=PIECE):
-        return pl.ds(pl.multiple_of(ch * CHUNK_TOKENS + v * PIECE + lo, 16), n)
+    def piece(ch):
+        return SIZES[ch] * QUERY_LEN // 4
+
+    def rows(ch, v, h=None):
+        n = piece(ch)
+        lo = STARTS[ch] * QUERY_LEN + v * n
+        if h is not None:
+            n = n // 2
+            lo = lo + h * n
+        return pl.ds(pl.multiple_of(lo, 16), n)
+
+    def quarter(ch):
+        return pl.ds(STARTS[ch] * QUERY_LEN // 4, piece(ch))
+
+    def eighth(ch):
+        return pl.ds(STARTS[ch] * QUERY_LEN // 8, piece(ch) // 2)
 
     def rotated(t, ds):
         if t == 0:
@@ -286,21 +303,21 @@
         if step == 1:
             v = at(g, 2)
             return [
-                (part.at[t, rows(ch, v, 0, HALF)], near.at[t, ch, 0], sem(t, ch, 0), g.up),
-                (part.at[t, rows(ch, v, HALF, HALF)], near.at[t, ch, 1], sem(t, ch, 1), g.dn),
+                (part.at[t, rows(ch, v, 0)], near.at[t, 0, eighth(ch)], sem(t, ch, 0), g.up),
+                (part.at[t, rows(ch, v, 1)], near.at[t, 1, eighth(ch)], sem(t, ch, 1), g.dn),
             ]
         if step == 2:
             return [
-                (part.at[t, rows(ch, at(g, 1))], mid.at[t, ch, 0], sem(t, ch, 2), g.up),
-                (part.at[t, rows(ch, at(g, 3))], mid.at[t, ch, 1], sem(t, ch, 3), g.dn),
+                (part.at[t, rows(ch, at(g, 1))], mid.at[t, 0, quarter(ch)], sem(t, ch, 2), g.up),
+                (part.at[t, rows(ch, at(g, 3))], mid.at[t, 1, quarter(ch)], sem(t, ch, 3), g.dn),
             ]
         if step == 3:
-            return [(mine.at[t, ch], other.at[t, ch], sem(t, ch, 4), g.pair)]
+            return [(mine.at[t, quarter(ch)], other.at[t, quarter(ch)], sem(t, ch, 4), g.pair)]
         if step == 4:
             v = rotated(t, rows(ch, g.u))
             return [(v, v, sem(t, ch, 5), g.up), (v, v, sem(t, ch, 6), g.dn)]
-        lo = rotated(t, rows(ch, at(g, 3), 0, HALF))
-        hi = rotated(t, rows(ch, at(g, 1), HALF, HALF))
+        lo = rotated(t, rows(ch, at(g, 3), 0))
+        hi = rotated(t, rows(ch, at(g, 1), 1))
         return [(lo, lo, sem(t, ch, 7), g.up), (hi, hi, sem(t, ch, 8), g.dn)]
 
     def reduce_start(t, g, ch, step):
@@ -311,7 +328,7 @@
         remote(v, v, i, dev).wait_recv()
 
     def chunk_rows(ch):
-        return pl.ds(pl.multiple_of(ch * CHUNK_TOKENS, 16), CHUNK_TOKENS)
+        return pl.ds(STARTS[ch] * QUERY_LEN, SIZES[ch] * QUERY_LEN)
 
     def sib_rot(ch):
         v = rot_g.at[chunk_rows(ch), lanes(k)]
@@ -319,36 +336,36 @@
 
     def partials(ch):
         ds = chunk_rows(ch)
-        of = pl.ds(ch * PER_CHUNK, PER_CHUNK)
+        of = pl.ds(STARTS[ch], SIZES[ch])
         for t, ref, basis in ((0, qa, ab), (1, qg, gb)):
             part[t, ds] = jnp.dot(
-                ref[of].reshape(CHUNK_TOKENS, TILE_I), basis[...], preferred_element_type=F32
+                ref[of].reshape(SIZES[ch] * QUERY_LEN, TILE_I), basis[...], preferred_element_type=F32
             ).astype(BF16)
         for t, g in kinds:
             reduce_start(t, g, ch, 1)
 
     def step2(ch):
         for t, g in kinds:
-            landed(near.at[t, ch, 0], sem(t, ch, 0), g.dn)
-            ds = rows(ch, at(g, 1), 0, HALF)
-            part[t, ds] = (part[t, ds].astype(F32) + near[t, ch, 0].astype(F32)).astype(BF16)
-            landed(near.at[t, ch, 1], sem(t, ch, 1), g.up)
-            ds = rows(ch, at(g, 3), HALF, HALF)
-            part[t, ds] = (part[t, ds].astype(F32) + near[t, ch, 1].astype(F32)).astype(BF16)
+            landed(near.at[t, 0, eighth(ch)], sem(t, ch, 0), g.dn)
+            ds = rows(ch, at(g, 1), 0)
+            part[t, ds] = (part[t, ds].astype(F32) + near[t, 0, eighth(ch)].astype(F32)).astype(BF16)
+            landed(near.at[t, 1, eighth(ch)], sem(t, ch, 1), g.up)
+            ds = rows(ch, at(g, 3), 1)
+            part[t, ds] = (part[t, ds].astype(F32) + near[t, 1, eighth(ch)].astype(F32)).astype(BF16)
             reduce_start(t, g, ch, 2)
 
     def step3(ch):
         for t, g in kinds:
-            landed(mid.at[t, ch, 0], sem(t, ch, 2), g.dn)
-            landed(mid.at[t, ch, 1], sem(t, ch, 3), g.up)
-            total = part[t, rows(ch, g.u)].astype(F32) + mid[t, ch, 0].astype(F32) + mid[t, ch, 1].astype(F32)
-            mine[t, ch] = total.astype(BF16)
+            landed(mid.at[t, 0, quarter(ch)], sem(t, ch, 2), g.dn)
+            landed(mid.at[t, 1, quarter(ch)], sem(t, ch, 3), g.up)
+            total = part[t, rows(ch, g.u)].astype(F32) + mid[t, 0, quarter(ch)].astype(F32) + mid[t, 1, quarter(ch)].astype(F32)
+            mine[t, quarter(ch)] = total.astype(BF16)
             reduce_start(t, g, ch, 3)
 
     def step4(ch):
         for t, g in kinds:
-            landed(other.at[t, ch], sem(t, ch, 4), g.pair)
-            total = (mine[t, ch].astype(F32) + other[t, ch].astype(F32)).astype(BF16)
+            landed(other.at[t, quarter(ch)], sem(t, ch, 4), g.pair)
+            total = (mine[t, quarter(ch)].astype(F32) + other[t, quarter(ch)].astype(F32)).astype(BF16)
             if t == 0:
                 rot_a[rows(ch, g.u)] = total
             else:
@@ -363,16 +380,16 @@
 
     def step6(ch):
         for t, g in reversed(kinds):
-            landed(rotated(t, rows(ch, at(g, 2), 0, HALF)), sem(t, ch, 7), g.dn)
-            landed(rotated(t, rows(ch, at(g, 2), HALF, HALF)), sem(t, ch, 8), g.up)
+            landed(rotated(t, rows(ch, at(g, 2), 0)), sem(t, ch, 7), g.dn)
+            landed(rotated(t, rows(ch, at(g, 2), 1)), sem(t, ch, 8), g.up)
             if t == 1:
                 sib_rot(ch).start()
 
     def make_panels(ch):
         v = rot_g.at[chunk_rows(ch), lanes(1 - k)]
         landed(v, sem(1, ch, 9), sib)
-        for i in range(PER_CHUNK):
-            ds = pl.ds(pl.multiple_of((ch * PER_CHUNK + i) * QUERY_LEN, QUERY_LEN), QUERY_LEN)
+        for i in range(SIZES[ch]):
+            ds = pl.ds((STARTS[ch] + i) * QUERY_LEN, QUERY_LEN)
             outer = lax.dot_general(
                 rot_g[ds], rot_a[ds], (((0,), (0,)), ((), ())), preferred_element_type=F32
             )
@@ -380,11 +397,11 @@
 
     def score(ch, h):
         mapped = jnp.dot(
-            tg[pl.ds(4 * h, 4)].reshape(4 * BLOCK, TILE_I), panels[ch % 2], preferred_element_type=F32
+            tg[pl.ds(4 * h, 4)].reshape(4 * BLOCK, TILE_I), panels[ch % 2, :, : SIZES[ch] * TILE_J], preferred_element_type=F32
         )
         acts = ta[pl.ds(4 * h, 4)].reshape(4 * BLOCK, TILE_J).astype(F32)
-        for i in range(PER_CHUNK):
-            q = ch * PER_CHUNK + i
+        for i in range(SIZES[ch]):
+            q = STARTS[ch] + i
             total = None
             for j in range(TILE_J // 128):
                 term = mapped[:, i * TILE_J + j * 128 : i * TILE_J + (j + 1) * 128] * acts[:, j * 128 : (j + 1) * 128]
@@ -417,7 +434,7 @@
 
     events = {
         "q0": query_pair, "q1": query_own, "t0": train_own, "qf0": query_near0, "qn1": query_pair_in,
-        "tp": train_pair_out, "tf0": train_near0, "qf1": query_near1, "qe": query_far,
+        "tp": train_pair_out, "tf0": train_near0, "qf1": query_near1, "qe": query_far, "qw": query_end,
         "tn1": train_pair, "tf1": train_near1, "te": train_far, "tw": train_end,
     }
     steps = {
@@ -435,31 +452,17 @@
         for j in range(4):
             blocks[4 * h + j] = turned[:, j * BLOCK : (j + 1) * BLOCK]
 
-    def to_row(d):
-        peer = (r + d) % ROWS
-        return remote(blocks.at[peer], first.at[d - 1], FIRST + d - 1, (peer, c))
-
-    for d in range(1, ROWS):
-        to_row(d).start()
-    total = blocks[r]
-    for d in range(1, ROWS):
-        landed(first.at[d - 1], FIRST + d - 1, ((r + ROWS - d) % ROWS, c))
-        total = total + first[d - 1]
-    total = total / D
-    for j in range(COLS):
-        split[j, :, :OWNED] = total[:, j * OWNED : (j + 1) * OWNED]
-
-    def to_col(d):
-        peer = (c + d) % COLS
-        return remote(split.at[peer], second.at[d - 1], SECOND + d - 1, (r, peer))
-
-    for d in range(1, COLS):
-        to_col(d).start()
-    total = split[c]
-    for d in range(1, COLS):
-        landed(second.at[d - 1], SECOND + d - 1, (r, (c + COLS - d) % COLS))
-        total = total + second[d - 1]
-    out_ref[...] = total[:, :OWNED]
+    row_moves = ((1, 2), (1, 1), (1, 3), (0, 2), (1, 0), (0, 1), (0, 3))
+
+    def row_peer(a, d):
+        return (xl + a) % 2 * 4 + (y + d) % 4
+
+    def to_row(i):
+        peer = row_peer(*row_moves[i])
+        return remote(blocks.at[peer], first.at[i], FIRST + i, (peer, c))
+
+    for i in range(ROWS - 1):
+        to_row(i).start()
 
     for g in queries + trains:
         g.wait_send()
@@ -467,19 +470,44 @@
         g.sib_wait_send()
     basis_copy.wait_send()
 
-    def drain(ch, carry):
+    for ch in range(CHUNKS):
         for t, g in kinds:
             for step in range(1, 6):
                 for a in reduce_copies(t, g, ch, step):
                     remote(*a).wait_send()
         sib_rot(ch).wait_send()
-        return carry
-
-    lax.fori_loop(0, CHUNKS, drain, 0)
-    for d in range(1, ROWS):
-        to_row(d).wait_send()
-    for d in range(1, COLS):
-        to_col(d).wait_send()
+
+    total = blocks[r]
+    for i in reversed(range(ROWS - 1)):
+        a, d = row_moves[i]
+        landed(first.at[i], FIRST + i, (row_peer(a, 4 - d), c))
+        total = total + first[i]
+    total = total / D
+    for j in range(COLS):
+        split[j, :, :OWNED] = total[:, j * OWNED : (j + 1) * OWNED]
+
+    col_moves = tuple((a, d, e) for a, d in ((1, 2),) + row_moves[1:] + ((0, 0),) for e in (1, 0) if (a, d, e) != (0, 0, 0))
+
+    def col_peer(a, d, e):
+        return (xh + a) % 2 * 8 + (z + d) % 4 * 2 + (k + e) % 2
+
+    def to_col(i):
+        peer = col_peer(*col_moves[i])
+        return remote(split.at[peer], second.at[i], SECOND + i, (r, peer))
+
+    for i in range(COLS - 1):
+        to_col(i).start()
+    for i in range(ROWS - 1):
+        to_row(i).wait_send()
+    total = split[c]
+    for i in reversed(range(COLS - 1)):
+        a, d, e = col_moves[i]
+        landed(second.at[i], SECOND + i, (r, col_peer(a, 4 - d, e)))
+        total = total + second[i]
+    out_ref[...] = total[:, :OWNED]
+
+    for i in range(COLS - 1):
+        to_col(i).wait_send()
 
 
 def shards(*args):
@@ -501,11 +529,11 @@
             vmem((2, TOKENS, TILE_J), BF16),
             vmem((TOKENS, TILE_J), BF16),
             vmem((TOKENS, TILE_I), BF16),
-            vmem((2, CHUNKS, 2, HALF, TILE_J), BF16),
-            vmem((2, CHUNKS, 2, PIECE, TILE_J), BF16),
-            vmem((2, CHUNKS, PIECE, TILE_J), BF16),
-            vmem((2, CHUNKS, PIECE, TILE_J), BF16),
-            vmem((2, TILE_I, PER_CHUNK * TILE_J), BF16),
+            vmem((2, 2, TOKENS // 8, TILE_J), BF16),
+            vmem((2, 2, TOKENS // 4, TILE_J), BF16),
+            vmem((2, TOKENS // 4, TILE_J), BF16),
+            vmem((2, TOKENS // 4, TILE_J), BF16),
+            vmem((2, TILE_I, max(SIZES) * TILE_J), BF16),
             vmem((2, 4 * BLOCK, 128), F32),
             vmem((ROWS, QUERIES, BLOCK), F32),
             vmem((ROWS - 1, QUERIES, BLOCK), F32),

time: 97.6 us -> 94.6 us (0.969)
  Pallas kernels: 96.2 us -> 93.2 us
    pallas_call x1, Pallas kernels: 96.2 us -> 93.2 us  [shards(): pl.pallas_call(kernel, out_shape=jax.ShapeDtypeStruct((QUERIES, OWNED), F...]
where the time goes in v4:
time: 94.6 us; the launch traced here: 94.5 us
  Pallas kernels  93.2 us (99%)
  local copies, waits for them, and re-layouts  1.28 us (1%)
    pallas_call x1, Pallas kernels, shards(): pl.pallas_call(kernel, out_shape=jax.ShapeDtypeStruct((QUERIES, OWNED), F...  93.2 us

profile of v4, /device:TPU:1, one launch (start us, length us, event | category | flops | bytes accessed | tf_op | source)
XLA Modules:
  0.0 94.5 jit_solution(15443043478743536910)
XLA Ops:
  0.0 93.2 %influence.1 = f32[8,20]{1,0:T(8,128)} custom-call(bf16[128,768]{1,0:T(8,128)(2,1)} %qa_ref.1, bf16[256,384]{1,0:T(8,128)(2,1)} %qg_ref.1, bf16[768,384]{1,0:T(8,128)(2,1)} %ab_ref.1, bf16[384,768]{1,0:T(8,128)(2,1)} %gb_ref.1, f32[768,384]{1,0:T(8,128)} %eig_ref.1, bf16[320,384]{1,0:T(8,128)(2,1)} %ta_ref.1, bf16[160,768]{1,0:T(8,128)(2,1)} %tg_ref.1), custom_call_target="tpu_custom_call" | custom-call | tf_op jit(solution)/shard_map/influence/pallas_call | solution.py:516
  93.2 1.3 %copy.9 = f32[8,20]{1,0:T(8,128)} copy(f32[8,20]{1,0:T(8,128)} %influence.1) | data formatting | bytes 1280

commit v5 on v4

--- a/solution.py
+++ b/solution.py
@@ -24,10 +24,10 @@
 STARTS = tuple(sum(SIZES[:ch]) for ch in range(CHUNKS))
 
 ORDER = (
-    "q0", "q1", "t0", "qf0", "tp", "qn1", "tf0", "qf1", "tn1", "qe", "qw", "P0", "P1", "P2",
-    "20", "P3", "21", "22", "30", "23", "31", "32", "40", "tf1", "33", "50", "41", "te",
-    "42", "60", "51", "N0", "43", "tw", "S0", "52", "61", "T0", "N1", "53", "S1", "62",
-    "T1", "63", "N2", "S2", "T2", "N3", "S3", "T3",
+    "q0", "q1", "t0", "qf0", "tp", "qn1", "tf0", "qf1", "tn1", "qe", "tx", "qw", "P0", "P1",
+    "P2", "20", "P3", "21", "22", "30", "23", "31", "32", "40", "33", "50", "41", "tf1",
+    "te", "42", "60", "51", "N0", "43", "tw", "S0", "52", "61", "T0", "N1", "53", "S1",
+    "62", "T1", "63", "N2", "S2", "T2", "N3", "S3", "T3",
 )
 
 MESH = pl.DeviceIdType.MESH
@@ -95,7 +95,8 @@
         return view
 
     class Gather:
-        def __init__(self, g, src, view, view_sib, n, base, sib_base):
+        def __init__(self, g, src, view, view_sib, n, base, sib_base, last="far1"):
+            self.last = last
             self.g, self.src, self.view, self.view_sib = g, src, view, view_sib
             self.n, self.base, self.sib_base = n, base, sib_base
             p, u = g.p, g.u
@@ -123,6 +124,9 @@
             if stage == "near1":
                 v = self.full(self.q1)
                 return [(v, v, b + 3, g.up), (v, v, b + 4, g.dn)]
+            if stage == "cross":
+                v = self.full(self.far[0])
+                return [(v, v, b + 7, g.pair)]
             i = 0 if stage == "far0" else 1
             lo, hi = self.half(self.low[i], 0), self.half(self.high[i], 1)
             return [(lo, lo, b + 5 + 2 * i, g.up), (hi, hi, b + 6 + 2 * i, g.dn)]
@@ -132,7 +136,7 @@
                 remote(*a).start()
 
         def wait_send(self):
-            for stage in ("pair", "near0", "near1", "far0", "far1"):
+            for stage in ("pair", "near0", "near1", "far0", self.last):
                 for a in self.copies(stage):
                     remote(*a).wait_send()
 
@@ -140,6 +144,8 @@
             b, g = self.base, self.g
             if stage == "pair":
                 got_ = [(self.full(self.q1), b, g.pair)]
+            elif stage == "cross":
+                got_ = [(self.full(self.far[1]), b + 7, g.pair)]
             elif stage in ("near0", "near1"):
                 i = 0 if stage == "near0" else 1
                 got_ = [
@@ -182,8 +188,8 @@
     half_q, half_t = QUERY_LEN // 2, BLOCK // 2
     g_qa = Gather(col_g, qa_ref, rows_of(qa, k, half_q), rows_of(qa, 1 - k, half_q), half_q, AG_A, SIB_A)
     g_qg = Gather(row_g, qg_ref, lanes_of(qg, k), lanes_of(qg, 1 - k), QUERY_LEN, AG_G, SIB_G)
-    g_ta = Gather(row_g, ta_ref, whole(ta), None, BLOCK, AG_TA, None)
-    g_tg = Gather(col_g, tg_ref, rows_of(tg, k, half_t), rows_of(tg, 1 - k, half_t), half_t, AG_TG, SIB_TG)
+    g_ta = Gather(row_g, ta_ref, whole(ta), None, BLOCK, AG_TA, None, "cross")
+    g_tg = Gather(col_g, tg_ref, rows_of(tg, k, half_t), rows_of(tg, 1 - k, half_t), half_t, AG_TG, SIB_TG, "cross")
     queries, trains = (g_qa, g_qg), (g_ta, g_tg)
 
     copies = [
@@ -205,6 +211,8 @@
         pl.semaphore_signal(barrier, inc=1, device_id=dev, device_id_type=MESH)
     for cp in copies:
         cp.start()
+    acc[...] = jnp.zeros_like(acc)
+    split[...] = jnp.zeros_like(split)
     pl.semaphore_wait(barrier, ROWS + COLS - 2)
 
     own_basis = gb.at[pl.ds(pl.multiple_of(k * TILE_J, TILE_J), TILE_J)]
@@ -337,11 +345,10 @@
     def partials(ch):
         ds = chunk_rows(ch)
         of = pl.ds(STARTS[ch], SIZES[ch])
-        for t, ref, basis in ((0, qa, ab), (1, qg, gb)):
+        for (t, g), ref, basis in zip(kinds, (qa, qg), (ab, gb)):
             part[t, ds] = jnp.dot(
                 ref[of].reshape(SIZES[ch] * QUERY_LEN, TILE_I), basis[...], preferred_element_type=F32
             ).astype(BF16)
-        for t, g in kinds:
             reduce_start(t, g, ch, 1)
 
     def step2(ch):
@@ -408,8 +415,6 @@
                 total = term if total is None else total + term
             acc[h, :, q : q + 1] = jnp.sum(total, axis=1, keepdims=True)
 
-    acc[...] = jnp.zeros_like(acc)
-    split[...] = jnp.zeros_like(split)
 
     def train_pair():
         for g in trains:
@@ -420,14 +425,18 @@
     def train_near1():
         for g in trains:
             g.wait("near1")
-            g.start("far1")
         g_tg.sib_start(4, 5)
 
+    def train_cross():
+        for g in trains:
+            g.wait("far0")
+            g.start("cross")
+        g_tg.sib_start(6)
+
     def train_far():
         for g in trains:
-            g.wait("far0")
-            g.wait("far1")
-        g_tg.sib_start(6, 7)
+            g.wait("cross")
+        g_tg.sib_start(7)
 
     def train_end():
         g_tg.sib_wait()
@@ -435,7 +444,7 @@
     events = {
         "q0": query_pair, "q1": query_own, "t0": train_own, "qf0": query_near0, "qn1": query_pair_in,
         "tp": train_pair_out, "tf0": train_near0, "qf1": query_near1, "qe": query_far, "qw": query_end,
-        "tn1": train_pair, "tf1": train_near1, "te": train_far, "tw": train_end,
+        "tn1": train_pair, "tf1": train_near1, "te": train_far, "tx": train_cross, "tw": train_end,
     }
     steps = {
         "P": partials, "2": step2, "3": step3, "4": step4, "5": step5, "6": step6,

time: 94.6 us -> 94.4 us (level)
  no operation moved by 1% of the time
where the time goes in v5:
time: 94.4 us; the launch traced here: 94.2 us
  Pallas kernels  92.9 us (98%)
  local copies, waits for them, and re-layouts  1.28 us (1%)
    pallas_call x1, Pallas kernels, shards(): pl.pallas_call(kernel, out_shape=jax.ShapeDtypeStruct((QUERIES, OWNED), F...  92.9 us

profile of v5, /device:TPU:1, one launch (start us, length us, event | category | flops | bytes accessed | tf_op | source)
XLA Modules:
  0.0 94.2 jit_solution(18397617356531590012)
XLA Ops:
  0.0 92.9 %influence.1 = f32[8,20]{1,0:T(8,128)} custom-call(bf16[128,768]{1,0:T(8,128)(2,1)} %qa_ref.1, bf16[256,384]{1,0:T(8,128)(2,1)} %qg_ref.1, bf16[768,384]{1,0:T(8,128)(2,1)} %ab_ref.1, bf16[384,768]{1,0:T(8,128)(2,1)} %gb_ref.1, f32[768,384]{1,0:T(8,128)} %eig_ref.1, bf16[320,384]{1,0:T(8,128)(2,1)} %ta_ref.1, bf16[160,768]{1,0:T(8,128)(2,1)} %tg_ref.1), custom_call_target="tpu_custom_call" | custom-call | tf_op jit(solution)/shard_map/influence/pallas_call | solution.py:525
  93.0 1.3 %copy.9 = f32[8,20]{1,0:T(8,128)} copy(f32[8,20]{1,0:T(8,128)} %influence.1) | data formatting | bytes 1280
